TPU v7x, 32 devices: a whole 2x2x4 slice. The times are simulated.
32 devices in a mesh: dp: 8 (over y, x, core), tensor: 4 (over z).
Axes of the slice: x: 2, y: 2, z: 4, core: 2. Of those that a mesh axis runs over, the one named last changes fastest.
Arguments:
- hidden_in: bfloat16 [32, 512, 768], P('dp'), may hold values from -6 to 6
- out_grad: bfloat16 [32, 512, 768], P('dp'), may hold values from -3 to 3
- segment_ids: int32 [32, 512], P('dp'), may hold values from 0 to 7, never falling along the last dimension, each value on 1 to 256 neighbouring positions
- step_count: int32 [1], replicated, may hold values from 1 to 199999
- qkv_state: float32 [3, 768, 3, 768], P(None, 'dp', None, 'tensor'), as said below
- qv_bias_state: float32 [3, 2, 12, 64], P(None, None, 'tensor', 'dp'), as said below
- out_state: float32 [3, 768, 768], P(None, 'tensor', 'dp'), as said below
- up_state: float32 [3, 768, 3072], P(None, 'dp', 'tensor'), as said below
- up_bias_state: float32 [3, 24, 128], P(None, 'tensor', 'dp'), as said below
- down_state: float32 [3, 3072, 768], P(None, 'tensor', 'dp'), as said below
- vector_state: float32 [3, 6, 768], P(None, None, 'dp'), as said below
Outputs:
- hidden_out: bfloat16 [32, 512, 768], P('dp')
- grad_in: bfloat16 [32, 512, 768], P('dp')
- grad_qkv: float32 [768, 3, 768], P('dp', None, 'tensor')
- grad_qv_bias: float32 [2, 12, 64], P(None, 'tensor', 'dp')
- grad_out: float32 [768, 768], P('tensor', 'dp')
- grad_up: float32 [768, 3072], P('dp', 'tensor')
- grad_up_bias: float32 [24, 128], P('tensor', 'dp')
- grad_down: float32 [3072, 768], P('tensor', 'dp')
- grad_vectors: float32 [6, 768], P(None, 'dp')
- new_qkv_state: float32 [2, 768, 3, 768], P(None, 'dp', None, 'tensor')
- new_qv_bias_state: float32 [2, 2, 12, 64], P(None, None, 'tensor', 'dp')
- new_out_state: float32 [2, 768, 768], P(None, 'tensor', 'dp')
- new_up_state: float32 [2, 768, 3072], P(None, 'dp', 'tensor')
- new_up_bias_state: float32 [2, 24, 128], P(None, 'tensor', 'dp')
- new_down_state: float32 [2, 3072, 768], P(None, 'tensor', 'dp')
- new_vector_state: float32 [2, 6, 768], P(None, None, 'dp')
- plan: float32 [3], replicated
Inputs may be any that keep to these rules, and one draw needn't show every extreme that they name: `segment_ids`: within each packed row the fragment numbers never fall; a token attends exactly to the tokens of its own row with the same number. `qkv_state`: index 2 (second moments) is positive. `qv_bias_state`: index 2 (second moments) is positive. `out_state`: index 2 (second moments) is positive. `up_state`: index 2 (second moments) is positive. `up_bias_state`: index 2 (second moments) is positive. `down_state`: index 2 (second moments) is positive. `vector_state`: index 2 (second moments) is positive.
All inputs are finite; a program needn't handle non-finite values.
Results may differ from a plain program's by a relative error of at most 0.023.
The roundings to bfloat16 on the way count: a program that leaves them out, or rounds other values in their place, can miss the bound.
Values may be sent and summed in bfloat16 or wider, within the bound.
No kernel may reach another device: no remote copies, remote signals or barrier semaphores. Data moves between devices by JAX's collectives and lax.ppermute only.
A program may use at most 192 MiB of HBM per device.

v0:
```python
import math
import jax
import jax.numpy as jnp
from jax import lax
from jax.sharding import PartitionSpec as P

HD = 64
norm_eps = 1e-05
beta_first = 0.9
beta_second = 0.999
warm_steps = 10000.0
total_steps = 200000.0


def layer_norm(value, gain, shift):
    center = value - jnp.mean(value, axis=-1, keepdims=True)
    spread = jnp.mean(center * center, axis=-1, keepdims=True)
    return center * lax.rsqrt(spread + norm_eps) * gain + shift


def gelu_exact(value):
    return 0.5 * value * (1.0 + lax.erf(value * 0.7071067811865476))


def scores_of(query, key_rows, segments):
    raw = jnp.einsum(
        "bqhd,bkhd->bhqk", query, key_rows, preferred_element_type=jnp.float32
    ) * HD ** (-0.5)
    same = segments[:, :, None] == segments[:, None, :]
    return jnp.where(same[:, None], raw, -1e30)


def contract_rows(left, right):
    return lax.dot_general(
        left, right, (((0,), (0,)), ((), ())), preferred_element_type=jnp.float32
    )


def contract_cols(left, right):
    return lax.dot_general(
        left, right, (((1,), (1,)), ((), ())), preferred_element_type=jnp.float32
    )


def moment_update(state, grad):
    moment_one = beta_first * state[1] + (1.0 - beta_first) * grad
    moment_two = beta_second * state[2] + (1.0 - beta_second) * grad * grad
    return jnp.stack([moment_one, moment_two])


def body(
    hidden_in,
    out_grad,
    segment_ids,
    step_count,
    qkv_state,
    qv_bias_state,
    out_state,
    up_state,
    up_bias_state,
    down_state,
    vector_state,
):
    bf = jnp.bfloat16
    fl = jnp.float32
    w_qkv, b_qv, w_out, w_up, b_up, w_down, vectors = (
        lax.all_gather(qkv_state[0].astype(bf), "dp", axis=0, tiled=True),
        lax.all_gather(qv_bias_state[0].astype(bf), "dp", axis=2, tiled=True),
        lax.all_gather(out_state[0].astype(bf), "dp", axis=1, tiled=True),
        lax.all_gather(up_state[0].astype(bf), "dp", axis=0, tiled=True),
        lax.all_gather(up_bias_state[0].astype(bf), "dp", axis=1, tiled=True),
        lax.all_gather(down_state[0].astype(bf), "dp", axis=1, tiled=True),
        lax.all_gather(vector_state[0].astype(bf), "dp", axis=1, tiled=True),
    )
    count, length, width_model = hidden_in.shape
    rows = count * length
    heads_local = b_qv.shape[1]
    head_width = heads_local * HD
    ff_local = w_up.shape[1]
    scale = HD ** (-0.5)
    plain = hidden_in.reshape(rows, width_model)
    cotangent = out_grad.reshape(rows, width_model)
    vec = vectors.astype(fl)
    proj = jnp.einsum("td,dcf->tcf", plain, w_qkv, preferred_element_type=fl)
    bias_f = b_qv.astype(fl).reshape(2, head_width)
    bias = jnp.stack([bias_f[0], jnp.zeros((head_width,), fl), bias_f[1]])
    proj_b = (proj + bias[None]).astype(bf)
    heads = proj_b.reshape(count, length, 3, heads_local, HD)
    query = heads[:, :, 0]
    key_rows = heads[:, :, 1]
    value_rows = heads[:, :, 2]
    scores = scores_of(query, key_rows, segment_ids)
    top = jnp.max(scores, axis=-1, keepdims=True)
    expd = jnp.exp(scores - top)
    denom = jnp.sum(expd, axis=-1, keepdims=True)
    log_total = top + jnp.log(denom)
    probs_b = (expd / denom).astype(bf)
    context = (
        jnp.einsum("bhqk,bkhd->bqhd", probs_b, value_rows, preferred_element_type=fl)
        .astype(bf)
        .reshape(rows, head_width)
    )
    attn_part = jnp.dot(context, w_out, preferred_element_type=fl)
    attn = lax.psum(attn_part.astype(jnp.bfloat16), "tensor").astype(jnp.float32)
    first, first_pull = jax.vjp(layer_norm, plain.astype(fl) + attn + vec[4], vec[0], vec[1])
    first_b = first.astype(bf)
    up = jnp.dot(first_b, w_up, preferred_element_type=fl) + b_up.astype(fl).reshape(ff_local)
    act, gelu_pull = jax.vjp(gelu_exact, up)
    act_b = act.astype(bf)
    ffn_part = jnp.dot(act_b, w_down, preferred_element_type=fl)
    ffn = lax.psum(ffn_part.astype(jnp.bfloat16), "tensor").astype(jnp.float32)
    out, second_pull = jax.vjp(layer_norm, first + ffn + vec[5], vec[2], vec[3])
    grad_r2, grad_g2, grad_b2 = second_pull(cotangent.astype(fl))
    grad_ffn = grad_r2.astype(bf)
    grad_down = contract_rows(act_b, grad_ffn)
    grad_act = contract_cols(grad_ffn, w_down)
    grad_up_b = gelu_pull(grad_act)[0].astype(bf)
    grad_wup = contract_rows(first_b, grad_up_b)
    grad_bup = jnp.sum(grad_up_b, axis=0, dtype=fl).reshape(b_up.shape)
    feed_part = contract_cols(grad_up_b, w_up)
    feed_back = lax.psum(feed_part.astype(jnp.bfloat16), "tensor").astype(jnp.float32)
    grad_first = grad_r2 + feed_back.astype(bf).astype(fl)
    grad_r1, grad_g1, grad_b1 = first_pull(grad_first)
    grad_attn = grad_r1.astype(bf)
    grad_wout = contract_rows(context, grad_attn)
    grad_context = (
        contract_cols(grad_attn, w_out).astype(bf).reshape(count, length, heads_local, HD)
    )
    again = scores_of(query, key_rows, segment_ids)
    probs = jnp.exp(again - log_total)
    probs_again = probs.astype(bf)
    grad_probs = jnp.einsum("bqhd,bkhd->bhqk", grad_context, value_rows, preferred_element_type=fl)
    grad_value = jnp.einsum("bhqk,bqhd->bkhd", probs_again, grad_context, preferred_element_type=fl)
    row_dot = jnp.sum(probs * grad_probs, axis=-1, keepdims=True)
    grad_scores = (probs * (grad_probs - row_dot)).astype(bf)
    grad_query = (
        jnp.einsum("bhqk,bkhd->bqhd", grad_scores, key_rows, preferred_element_type=fl) * scale
    )
    grad_key = jnp.einsum("bhqk,bqhd->bkhd", grad_scores, query, preferred_element_type=fl) * scale
    grad_proj = (
        jnp.stack([grad_query, grad_key, grad_value], axis=2)
        .astype(bf)
        .reshape(rows, 3, head_width)
    )
    proj_sums = jnp.sum(grad_proj, axis=0, dtype=fl)
    grad_bqv = jnp.stack([proj_sums[0], proj_sums[2]]).reshape(2, heads_local, HD)
    grad_wqkv = jnp.einsum("td,tcf->dcf", plain, grad_proj, preferred_element_type=fl)
    input_part = jnp.einsum("tcf,dcf->td", grad_proj, w_qkv, preferred_element_type=fl)
    vec_part = jnp.stack(
        [grad_g1, grad_b1, grad_g2, grad_b2, jnp.sum(grad_r1, axis=0), jnp.sum(grad_r2, axis=0)]
    )
    input_back = lax.psum(input_part.astype(jnp.bfloat16), "tensor").astype(jnp.float32)
    grad_in = (grad_r1 + input_back.astype(bf).astype(fl)).astype(bf).reshape(hidden_in.shape)
    hidden_out = out.astype(bf).reshape(hidden_in.shape)
    summed = (
        lax.psum_scatter(grad_wqkv, "dp", scatter_dimension=0, tiled=True),
        lax.psum_scatter(grad_bqv, "dp", scatter_dimension=2, tiled=True),
        lax.psum_scatter(grad_wout, "dp", scatter_dimension=1, tiled=True),
        lax.psum_scatter(grad_wup, "dp", scatter_dimension=0, tiled=True),
        lax.psum_scatter(grad_bup, "dp", scatter_dimension=1, tiled=True),
        lax.psum_scatter(grad_down, "dp", scatter_dimension=1, tiled=True),
        lax.psum_scatter(vec_part, "dp", scatter_dimension=1, tiled=True),
    )
    steps_f = step_count[0].astype(fl)
    factor = jnp.minimum(steps_f / warm_steps, (total_steps - steps_f) / (total_steps - warm_steps))
    fix_first = 1.0 - jnp.exp(steps_f * math.log(beta_first))
    fix_second = 1.0 - jnp.exp(steps_f * math.log(beta_second))
    states = (
        qkv_state,
        qv_bias_state,
        out_state,
        up_state,
        up_bias_state,
        down_state,
        vector_state,
    )
    news = tuple((moment_update(s, g) for s, g in zip(states, summed)))
    plan = jnp.stack([factor, fix_first, fix_second])
    return (
        hidden_out,
        grad_in,
        summed[0],
        summed[1],
        summed[2],
        summed[3],
        summed[4],
        summed[5],
        summed[6],
        news[0],
        news[1],
        news[2],
        news[3],
        news[4],
        news[5],
        news[6],
        plan,
    )


def solution(mesh):
    return jax.shard_map(
        body,
        mesh=mesh,
        in_specs=(
            P("dp", None, None),
            P("dp", None, None),
            P("dp", None),
            P(),
            P(None, "dp", None, "tensor"),
            P(None, None, "tensor", "dp"),
            P(None, "tensor", "dp"),
            P(None, "dp", "tensor"),
            P(None, "tensor", "dp"),
            P(None, "tensor", "dp"),
            P(None, None, "dp"),
        ),
        out_specs=(
            P("dp", None, None),
            P("dp", None, None),
            P("dp", None, "tensor"),
            P(None, "tensor", "dp"),
            P("tensor", "dp"),
            P("dp", "tensor"),
            P("tensor", "dp"),
            P("tensor", "dp"),
            P(None, "dp"),
            P(None, "dp", None, "tensor"),
            P(None, None, "tensor", "dp"),
            P(None, "tensor", "dp"),
            P(None, "dp", "tensor"),
            P(None, "tensor", "dp"),
            P(None, "tensor", "dp"),
            P(None, None, "dp"),
            P(),
        ),
        check_vma=False,
    )
```

profile of v0, /device:TPU:0, one launch (start us, length us, event | category | flops | bytes accessed | tf_op | source)
XLA Modules:
  0.0 760.8 jit_solution(6386560561636301362)
XLA Ops:
  9.0 10.6 %all-gather.1 = bf16[1,2,3,64]{2,1,0,3:T(2,128)(2,1)S(1)} all-gather(bf16[1,2,3,8]{2,1,0,3:T(2,128)(2,1)S(1)} %copy.181), channel_id=3, replica_groups=mesh['dp'=8,'tensor'=4] {'dp'}, dimensions={3}, use_global_device_ids=true | all-gather | bytes 864 | tf_op jit(solution)/shard_map/all_gather | solution.py:68
  22.8 11.3 %all-gather.2 = bf16[1,192,768]{1,0,2:T(2,128)(2,1)} all-gather(bf16[1,192,96]{1,0,2:T(2,128)(2,1)S(1)} %copy.142), channel_id=4, replica_groups=mesh['dp'=8,'tensor'=4] {'dp'}, dimensions={2}, use_global_device_ids=true | all-gather | bytes 331776 | tf_op jit(solution)/shard_map/all_gather | solution.py:69
  34.1 2.2 copy.143
  36.3 2.3 broadcast_compare_fusion
  38.6 15.8 %all-gather = bf16[1,768,3,192]{3,2,0,1:T(4,128)(2,1)} all-gather(bf16[1,96,3,192]{3,2,0,1:T(4,128)(2,1)} %copy.132), channel_id=2, replica_groups=mesh['dp'=8,'tensor'=4] {'dp'}, dimensions={1}, use_global_device_ids=true | all-gather | bytes 995328 | tf_op jit(solution)/shard_map/all_gather | solution.py:67
  54.4 3.4 copy.133
  57.9 3.2 fusion.74
  61.2 1.7 add_convert_fusion.5
  62.9 6.2 reshape.215
  69.1 2.4 fusion.69
  71.5 4.4 fusion.73
  76.0 1.8 fusion
  77.8 2.8 copy-done
  80.7 2.3 fusion.22
  84.7 2.7 convolution_convert_fusion.2
  87.5 1.6 slice.205
  89.3 1.6 slice.204
  93.2 8.7 %all-gather.5 = bf16[1,6,128]{1,0,2:T(2,128)(2,1)S(1)} all-gather(bf16[1,6,16]{1,0,2:T(2,128)(2,1)} %copy.145), channel_id=7, replica_groups=mesh['dp'=8,'tensor'=4] {'dp'}, dimensions={2}, use_global_device_ids=true | all-gather | bytes 1728 | tf_op jit(solution)/shard_map/all_gather | solution.py:71
  103.2 10.8 %all-gather.3 = bf16[1,6,768]{1,0,2:T(2,128)(2,1)S(1)} all-gather(bf16[1,6,96]{1,0,2:T(2,128)(2,1)S(1)} %copy.185), channel_id=5, replica_groups=mesh['dp'=8,'tensor'=4] {'dp'}, dimensions={2}, use_global_device_ids=true | all-gather | bytes 10368 | tf_op jit(solution)/shard_map/all_gather | solution.py:73
  114.4 13.0 %slice_reduce_fusion.1 = (f32[768]{0:T(1024)S(1)}, f32[768]{0:T(1024)S(1)}, f32[768]{0:T(1024)S(1)}, f32[768]{0:T(1024)S(1)}, f32[768]{0:T(1024)S(1)}, /*index=5*/f32[768]{0:T(1024)S(1)}) fusion(f32[1,6,768]{1,0,2:T(1,128)S(1)} %convert_element_type.169), kind=kLoop, calls=%fused_computation.78 | loop fusion | bytes 36864 | tf_op jit(solution)/shard_map/slice | solution.py:112
  127.4 81.6 %all-reduce.6.cloned.1.call-done = bf16[2048,768]{1,0:T(8,128)(2,1)} async-done(((bf16[2048,768]{1,0:T(8,128)(2,1)}), bf16[2048,768]{1,0:T(8,128)(2,1)}) %all-reduce.6.cloned.1.call-update) | async-done | bytes 3145744 | tf_op jit(solution)/shard_map/psum | solution.py:104
  209.0 3.1 fusion.11
  212.1 3.7 multiply_reduce_fusion.4
  215.8 7.4 multiply_convert_fusion.1
  223.3 6.2 convolution_convert_fusion.1
  229.7 120.0 %all-reduce.8.cloned.1.call-done = bf16[2048,768]{1,0:T(8,128)(2,1)} async-done(((bf16[2048,768]{1,0:T(8,128)(2,1)}), bf16[2048,768]{1,0:T(8,128)(2,1)}) %all-reduce.8.cloned.1.call-update) | async-done | bytes 3145744 | tf_op jit(solution)/shard_map/psum | solution.py:111
  349.7 4.8 fusion.67
  356.4 3.0 fusion.7
  359.5 4.3 fusion.66
  363.8 5.9 convert_reduce_fusion.1
  369.7 1.7 copy-done.35
  371.5 4.0 convolution_convert_fusion
  376.4 8.0 %fusion.60 = f32[768,768]{0,1:T(8,128)} fusion(bf16[2048,768]{1,0:T(8,128)(2,1)} %copy-done.36, f32[2048,768]{1,0:T(8,128)} %copy-done.2, f32[2048]{0:T(1024)S(1)} %negate_multiply_fusion.1), kind=kOutput, calls=%fused_computation.147 | convolution fusion | flops 2419064832 | bytes 11804672 | tf_op jit(solution)/shard_map/dot_general | solution.py:34
  384.5 8.0 %fusion.61 = f32[768,768]{1,0:T(8,128)} fusion(bf16[2048,768]{1,0:T(8,128)(2,1)} %copy-done.35, f32[2048,768]{1,0:T(8,128)} %get-tuple-element.123, f32[768]{0:T(1024)} %copy-done.24, f32[768]{0:T(1024)} %copy-done.22, f32[2048]{0:T(1024)S(1)} %fusion.49), kind=kOutput, calls=%fused_computation.148 | convolution fusion | flops 2422210560 | bytes 11810816 | tf_op jit(solution)/shard_map/dot_general | solution.py:34
  392.8 102.9 %all-reduce.10.cloned.1.call-done = bf16[2048,768]{1,0:T(8,128)(2,1)} async-done(((bf16[2048,768]{1,0:T(8,128)(2,1)}), bf16[2048,768]{1,0:T(8,128)(2,1)}) %all-reduce.10.cloned.1.call-update) | async-done | bytes 3145744 | tf_op jit(solution)/shard_map/psum | solution.py:121
  495.7 8.0 %multiply_reduce_fusion.1 = (f32[768]{0:T(1024)}, f32[2048]{0:T(1024)S(1)}, f32[768]{0:T(1024)}, f32[768]{0:T(1024)}) fusion(f32[2048,768]{1,0:T(8,128)} %get-tuple-element.123, f32[2048]{0:T(1024)S(1)} %fusion.49, bf16[2048,768]{1,0:T(8,128)(2,1)} %all-reduce.10.cloned.1.call-done, f32[2048,768]{1,0:T(8,128)} %copy-done.2, ...), kind=kLoop, calls=%fused_computation.19 | loop fusion | flops 17297152 | bytes 15765504 | tf_op jit(solution)/shard_map/transpose(jvp())/reduce_sum | solution.py:18
  503.7 6.1 fusion.65
  509.8 2.6 copy-done.3
  512.4 2.2 convolution_convert_fusion.3
  514.7 3.0 reshape.218
  517.6 8.3 %multiply_reduce_fusion = (f32[4,3,512]{2,1,0:T(4,128)S(1)}, f32[4,3,512,512]{2,3,1,0:T(8,128)S(1)}) fusion(f32[4,3,512,512]{2,3,1,0:T(8,128)} %copy-done, f32[4,3,512]{2,1,0:T(4,128)S(1)} %log_add_fusion, bf16[4,512,1,3,64]{1,0,4,3,2:T(4,128)(2,1)} %copy-done.11, bf16[4,512,3,64]{1,0,3,2:T(4,128)(2,1)} %reshape.218), kind=kOutput, calls=%fused_computation.1 | convolution fusion | flops 412084224 | bytes 26787840 | tf_op jit(solution)/shard_map/bqhd,bkhd->bhqk/dot_general | solution.py:132
  526.0 6.9 multiply_convert_fusion
  532.9 2.6 copy-done.1
  536.6 1.5 copy.149
  538.1 3.2 stack.101
  541.3 5.1 fusion.21
  546.3 1.5 copy.151
  547.8 2.8 stack.102
  550.6 2.1 constant_dynamic-update-slice_fusion.2
  552.8 5.6 convolution_bitcast_fusion
  558.4 7.7 %fusion.17 = bf16[4,512,3,64]{1,3,2,0:T(8,128)(2,1)} fusion(f32[4,3,512,512]{2,3,1,0:T(8,128)} %copy-done, f32[4,3,512]{2,1,0:T(4,128)S(1)} %log_add_fusion, bf16[4,512,3,64]{1,0,3,2:T(4,128)(2,1)} %reshape.218), kind=kOutput, calls=%fused_computation.53 | convolution fusion | flops 409337856 | bytes 14180352 | tf_op jit(solution)/shard_map/bhqk,bqhd->bkhd/dot_general | solution.py:133
  566.2 2.1 constant_dynamic-update-slice_fusion.1
  568.3 2.6 copy.154
  570.9 2.8 stack.103
  573.7 2.1 constant_dynamic-update-slice_fusion
  575.8 5.8 fusion.75
  581.7 2.8 copy.179
  585.8 6.2 bitcast_convert_fusion
  595.1 1.2 dynamic-slice
  601.6 14.3 %all-reduce = f32[2,3,64]{2,1,0:T(4,128)S(1)} all-reduce(f32[2,3,64]{2,1,0:T(4,128)S(1)} %reshape.220), channel_id=10, replica_groups=mesh['dp'=8,'tensor'=4] {'dp'}, use_global_device_ids=true, to_apply=%region_17.18.clone | all-reduce | flops 384 | bytes 3072
  623.8 19.7 %reduce-scatter.20.cloned.1.call-done = f32[96,576]{1,0:T(8,128)} async-done(((f32[768,576]{1,0:T(8,128)}), f32[96,576]{1,0:T(8,128)}) %reduce-scatter.20.cloned.1.call-update) | async-done | bytes 221200
  644.8 67.8 %all-reduce.12.cloned.1.call-done = bf16[2048,768]{1,0:T(8,128)(2,1)} async-done(((bf16[2048,768]{1,0:T(8,128)(2,1)}), bf16[2048,768]{1,0:T(8,128)(2,1)}) %all-reduce.12.cloned.1.call-update) | async-done | bytes 3145744 | tf_op jit(solution)/shard_map/psum | solution.py:152
  712.5 5.4 add_reduce_fusion
  721.0 31.0 %reduce-scatter.26.cloned.1.call-done = f32[96,6]{1,0:T(8,128)} async-done(((f32[768,6]{1,0:T(8,128)}), f32[96,6]{1,0:T(8,128)}) %reduce-scatter.26.cloned.1.call-update) | async-done | bytes 2320
  (180 shorter events, 36.6 us)
Async XLA Ops:
  8.0 49.9 %copy-start.6 = (bf16[4,512,768]{2,1,0:T(8,128)(2,1)S(1)}, bf16[4,512,768]{2,1,0:T(8,128)(2,1)}, u32[]{:S(2)}) copy-start(bf16[4,512,768]{2,1,0:T(8,128)(2,1)} %param.11) | copy-start | bytes 9437188
  8.0 200.9 %all-reduce.6.cloned.1.call-start = ((), (), s32[]{:S(2)}) async-start(), calls=%async_computation.6 | async-start | bytes 6291456 | tf_op jit(solution)/shard_map/psum | solution.py:104
  71.5 4.4 copy-start.9
  71.5 4.4 copy-start.12
  71.5 6.3 copy-start.11
  76.0 4.7 copy-start
  76.0 4.7 copy-start.16
  77.8 5.3 copy-start.18
  83.9 0.9 copy-start.8
  87.5 128.3 %all-gather.10.cloned.1.call-start = ((), (), s32[]{:S(2)}) async-start(), calls=%async_computation.12 | async-start | bytes 1327104 | tf_op jit(solution)/shard_map/all_gather | solution.py:70
  89.2 134.1 %all-gather.12.cloned.1.call-start = ((), (), s32[]{:S(2)}) async-start(), calls=%async_computation.13 | async-start | bytes 1327104 | tf_op jit(solution)/shard_map/all_gather | solution.py:72
  90.9 258.8 %all-reduce.8.cloned.1.call-start = ((), (), s32[]{:S(2)}) async-start(), calls=%async_computation.7 | async-start | bytes 6291456 | tf_op jit(solution)/shard_map/psum | solution.py:111
  127.3 222.4 %copy-start.22 = (f32[768]{0:T(1024)}, f32[768]{0:T(1024)S(1)}, u32[]{:S(2)}) copy-start(f32[768]{0:T(1024)S(1)} %get-tuple-element.111) | copy-start | bytes 9220
  127.3 222.4 %copy-start.24 = (f32[768]{0:T(1024)}, f32[768]{0:T(1024)S(1)}, u32[]{:S(2)}) copy-start(f32[768]{0:T(1024)S(1)} %get-tuple-element.110) | copy-start | bytes 9220
  208.9 3.2 copy-start.7
  215.8 7.5 copy-start.20
  223.3 6.2 copy-start.36
  229.5 266.2 %all-reduce.10.cloned.1.call-start = ((), (), s32[]{:S(2)}) async-start(), calls=%async_computation.8 | async-start | bytes 6291456 | tf_op jit(solution)/shard_map/psum | solution.py:121
  354.5 1.9 copy-start.4
  356.4 7.4 slice-start
  359.4 4.3 copy-start.34
  359.4 4.3 slice-start.1
  363.8 6.0 copy-start.2
  363.8 7.7 %copy-start.33 = (bf16[1,768,768]{2,1,0:T(8,128)(2,1)S(1)}, bf16[1,768,768]{2,1,0:T(8,128)(2,1)}, u32[]{:S(2)}) copy-start(bf16[1,768,768]{2,1,0:T(8,128)(2,1)} %all-gather.10.cloned.1.call-done) | copy-start | bytes 3538948
  369.7 1.8 copy-start.35
  375.5 222.1 %reduce-scatter.24.cloned.1.call-start = ((), (), s32[]{:S(2)}) async-start(), calls=%async_computation.16 | async-start | bytes 73728
  376.3 8.1 %copy-start.17 = (f32[4,3,512]{2,1,0:T(4,128)S(1)}, f32[4,3,512]{2,1,0:T(4,128)}, u32[]{:S(2)}) copy-start(f32[4,3,512]{2,1,0:T(4,128)} %copy-done.16) | copy-start | bytes 73732
  376.4 8.1 %copy-start.19 = (f32[4,3,512]{2,1,0:T(4,128)S(1)}, f32[4,3,512]{2,1,0:T(4,128)}, u32[]{:S(2)}) copy-start(f32[4,3,512]{2,1,0:T(4,128)} %copy-done.18) | copy-start | bytes 73732
  376.4 241.5 %reduce-scatter.18.cloned.1.call-start = ((), (), s32[]{:S(2)}) async-start(), calls=%async_computation.11 | async-start | bytes 2654208 | tf_op jit(solution)/shard_map/reduce_scatter | solution.py:161
  384.4 235.6 %reduce-scatter.16.cloned.1.call-start = ((), (), s32[]{:S(2)}) async-start(), calls=%async_computation.10 | async-start | bytes 2654208 | tf_op jit(solution)/shard_map/reduce_scatter | solution.py:159
  384.5 111.2 %copy-start.23 = (f32[768]{0:T(1024)S(1)}, f32[768]{0:T(1024)}, u32[]{:S(2)}) copy-start(f32[768]{0:T(1024)} %copy-done.22) | copy-start | bytes 9220
  392.5 111.2 %copy-start.21 = (f32[2048]{0:T(1024)S(1)}, f32[2048]{0:T(1024)}, u32[]{:S(2)}) copy-start(f32[2048]{0:T(1024)} %copy-done.20) | copy-start | bytes 24580
  392.6 229.5 %reduce-scatter.22.cloned.1.call-start = ((), (), s32[]{:S(2)}) async-start(), calls=%async_computation.15 | async-start | bytes 884736
  495.7 8.0 %copy-start.5 = (bf16[2048,768]{1,0:T(8,128)(2,1)S(1)}, bf16[2048,768]{1,0:T(8,128)(2,1)}, u32[]{:S(2)}) copy-start(bf16[2048,768]{1,0:T(8,128)(2,1)} %all-reduce.10.cloned.1.call-done) | copy-start | bytes 9437188
  509.8 2.6 copy-start.3
  526.0 9.5 %copy-start.13 = (bf16[4,512,1,3,64]{1,0,4,3,2:T(4,128)(2,1)S(1)}, bf16[4,512,1,3,64]{1,0,4,3,2:T(4,128)(2,1)}, u32[]{:S(2)}) copy-start(bf16[4,512,1,3,64]{1,0,4,3,2:T(4,128)(2,1)} %copy-done.12) | copy-start | bytes 2359300
  532.9 2.6 copy-start.1
  566.2 77.4 %reduce-scatter.20.cloned.1.call-start = ((), (), s32[]{:S(2)}) async-start(), calls=%async_computation.14 | async-start | bytes 2211840
  584.5 128.0 %all-reduce.12.cloned.1.call-start = ((), (), s32[]{:S(2)}) async-start(), calls=%async_computation.9 | async-start | bytes 6291456 | tf_op jit(solution)/shard_map/psum | solution.py:152
  585.8 8.3 %copy-start.27 = (f32[768]{0:T(1024)S(1)}, f32[768]{0:T(1024)}, u32[]{:S(2)}) copy-start(f32[768]{0:T(1024)} %convert_reduce_fusion) | copy-start | bytes 9220
  585.8 11.7 %copy-start.25 = (f32[768]{0:T(1024)S(1)}, f32[768]{0:T(1024)}, u32[]{:S(2)}) copy-start(f32[768]{0:T(1024)} %get-tuple-element.104) | copy-start | bytes 9220
  585.8 15.2 %copy-start.26 = (f32[768]{0:T(1024)S(1)}, f32[768]{0:T(1024)}, u32[]{:S(2)}) copy-start(f32[768]{0:T(1024)} %get-tuple-element.107) | copy-start | bytes 9220
  592.1 9.0 %copy-start.10 = (bf16[2048,3,192]{0,2,1:T(8,128)(2,1)S(1)}, bf16[2048,3,192]{0,2,1:T(8,128)(2,1)}, u32[]{:S(2)}) copy-start(bf16[2048,3,192]{0,2,1:T(8,128)(2,1)} %constant_dynamic-update-slice_fusion) | copy-start | bytes 7077892
  592.1 31.0 %copy-start.15 = (f32[3,192,96]{2,1,0:T(8,128)S(1)}, f32[3,192,96]{2,1,0:T(8,128)}, u32[]{:S(2)}) copy-start(f32[3,192,96]{2,1,0:T(8,128)} %param.17) | copy-start | bytes 663556
  592.1 159.8 %reduce-scatter.26.cloned.1.call-start = ((), (), s32[]{:S(2)}) async-start(), calls=%async_computation.17 | async-start | bytes 442368
  598.4 119.6 %copy-start.28 = (f32[6,16]{1,0:T(8,128)}, f32[6,16]{1,0:T(8,128)S(1)}, u32[]{:S(2)}) copy-start(f32[6,16]{1,0:T(8,128)S(1)} %copy.176) | copy-start | bytes 1156
  616.6 101.3 %copy-start.30 = (f32[2,3,8]{2,0,1:T(2,128)}, f32[2,3,8]{2,0,1:T(2,128)S(1)}, u32[]{:S(2)}) copy-start(f32[2,3,8]{2,0,1:T(2,128)S(1)} %get-tuple-element.115) | copy-start | bytes 580
  623.1 94.8 %copy-start.14 = (f32[192,96]{1,0:T(8,128)}, f32[192,96]{1,0:T(8,128)S(1)}, u32[]{:S(2)}) copy-start(f32[192,96]{1,0:T(8,128)S(1)} %copy.174) | copy-start | bytes 221188
  644.7 73.2 %copy-start.31 = (f32[1,768]{1,0:T(1,128)S(1)}, f32[1,768]{1,0:T(1,128)}, u32[]{:S(2)}) copy-start(f32[1,768]{1,0:T(1,128)} %reshape.225) | copy-start | bytes 9220
  644.7 108.1 %copy-start.32 = (f32[3,6,96]{2,1,0:T(8,128)S(1)}, f32[3,6,96]{2,1,0:T(8,128)}, u32[]{:S(2)}) copy-start(f32[3,6,96]{2,1,0:T(8,128)} %param.21) | copy-start | bytes 20740
  752.8 0.6 copy-start.29
Sparse Core Ops, SparseCore 0:
  87.6 121.2 all-reduce.5
  229.6 120.0 all-reduce.7
  375.6 120.0 all-reduce.9
  592.2 120.2 all-reduce.11
Sparse Core Ops, SparseCore 1:
  90.4 25.2 all-gather.9
  118.0 23.8 all-gather.11
  379.6 32.5 reduce-scatter.23
  416.1 42.2 reduce-scatter.17
  462.2 42.2 reduce-scatter.15
  566.2 33.9 reduce-scatter.21
  603.5 40.0 reduce-scatter.19
  719.0 32.9 reduce-scatter.25
where the time goes:
time: 772 us; the launch traced here: 761 us
  waiting for transfers between devices  423 us (55%)
  matrix products  94.3 us (12%)
  local copies, waits for them, and re-layouts  90.2 us (12%)
  blocking collectives  71.4 us (9%)
  other arithmetic  63 us (8%)
  between operations  17.6 us (2%)
    psum x1, waiting for transfers between devices, body(): ffn = lax.psum(ffn_part.astype(jnp.bfloat16), 'tensor').astype(jnp.float32)  120 us
    psum x1, waiting for transfers between devices, body(): lax.psum(feed_part.astype(jnp.bfloat16), 'tensor').astype(jnp.float32)  103 us
    psum x1, waiting for transfers between devices, body(): lax.psum(attn_part.astype(jnp.bfloat16), 'tensor').astype(jnp.float32)  81.6 us
    psum x1, waiting for transfers between devices, body(): lax.psum(input_part.astype(jnp.bfloat16), 'tensor').astype(jnp.float32)  67.8 us
    unnamed x16, waiting for transfers between devices  50.9 us
    unnamed x98, local copies, waits for them, and re-layouts  29.5 us
    reduce_sum x4, other arithmetic, layer_norm(): center = value - jnp.mean(value, axis=-1, keepdims=True)  18.3 us
    dot_general x2, matrix products, contract_rows(): lax.dot_general(left, right, (((0,), (0,)), ((), ())), preferred_element_...  16 us
  transfers between devices with their start and end apart: 12, of which 6 were waited for; matrix products, arithmetic and copies ran while one was open for 21% of the time, Pallas kernels for 0%

commit v1 on v0

--- a/solution.py
+++ b/solution.py
@@ -1,3 +1,4 @@
+import functools
 import math
 import jax
 import jax.numpy as jnp
@@ -10,6 +11,35 @@
 beta_second = 0.999
 warm_steps = 10000.0
 total_steps = 200000.0
+
+
+def targets_bind(matrix, d0):
+    matrix = jnp.moveaxis(matrix, 0, d0)
+    reply = matrix.shape
+    r2 = matrix.reshape(*reply[:d0], reply[d0] * reply[d0 + 1], *reply[d0 + 2 :])
+    return r2
+
+
+def search_ways(work_x, group_axis):
+    spare, val = (lax.axis_size(group_axis), lax.axis_index(group_axis))
+    p_next, mid_arr = (work_x[None], 1)
+    while mid_arr < spare:
+        t1 = tuple(((dev_i, dev_i ^ mid_arr) for dev_i in range(spare)))
+        q_next = lax.ppermute(p_next, group_axis, t1)
+        wide_out = val & mid_arr == 0
+        p_next = jnp.concatenate(
+            [jnp.where(wide_out, p_next, q_next), jnp.where(wide_out, q_next, p_next)]
+        )
+        mid_arr *= 2
+    return p_next
+
+
+def rings_expand(q_in, panel, dim_at):
+    opened = targets_bind(search_ways(q_in, panel), dim_at)
+    return opened
+
+
+point_words_on = functools.partial(rings_expand, panel="dp", dim_at=0)
 
 
 def layer_norm(value, gain, shift):
@@ -64,7 +94,7 @@
     bf = jnp.bfloat16
     fl = jnp.float32
     w_qkv, b_qv, w_out, w_up, b_up, w_down, vectors = (
-        lax.all_gather(qkv_state[0].astype(bf), "dp", axis=0, tiled=True),
+        point_words_on(qkv_state[0].astype(bf)),
         lax.all_gather(qv_bias_state[0].astype(bf), "dp", axis=2, tiled=True),
         lax.all_gather(out_state[0].astype(bf), "dp", axis=1, tiled=True),
         lax.all_gather(up_state[0].astype(bf), "dp", axis=0, tiled=True),

time: 772 us -> 776 us (level)
  blocking collectives: 71.4 us -> 55.7 us
  waiting for transfers between devices: 423 us -> 438 us
    all_gather x1 -> x0, blocking collectives: 15.8 us -> none  [body(): lax.all_gather(qkv_state[0].astype(bf), 'dp', axis=0, tiled=True)]
    ppermute x0 -> x3, waiting for transfers between devices: none -> 13.5 us  [search_ways(): q_next = lax.ppermute(p_next, group_axis, t1)]
    unnamed x98 -> x104, local copies, waits for them, and re-layouts: 29.5 us -> 30.1 us
  transfers between devices with their start and end apart: 12 -> 15, of which waited for: 6 -> 7; matrix products, arithmetic and copies ran while one was open for 21% -> 22% of each run, Pallas kernels for 0% -> 0%
where the time goes in v1:
time: 776 us; the launch traced here: 766 us
  waiting for transfers between devices  438 us (56%)
  matrix products  96.2 us (12%)
  local copies, waits for them, and re-layouts  90.2 us (12%)
  other arithmetic  65.3 us (8%)
  blocking collectives  55.7 us (7%)
  between operations  17.6 us (2%)
    psum x1, waiting for transfers between devices, body(): ffn = lax.psum(ffn_part.astype(jnp.bfloat16), 'tensor').astype(jnp.float32)  120 us
    psum x1, waiting for transfers between devices, body(): lax.psum(feed_part.astype(jnp.bfloat16), 'tensor').astype(jnp.float32)  103 us
    psum x1, waiting for transfers between devices, body(): lax.psum(attn_part.astype(jnp.bfloat16), 'tensor').astype(jnp.float32)  82.3 us
    psum x1, waiting for transfers between devices, body(): lax.psum(input_part.astype(jnp.bfloat16), 'tensor').astype(jnp.float32)  67.7 us
    unnamed x16, waiting for transfers between devices  50.9 us
    unnamed x104, local copies, waits for them, and re-layouts  30.1 us
    reduce_sum x4, other arithmetic, layer_norm(): center = value - jnp.mean(value, axis=-1, keepdims=True)  18.4 us
    dot_general x2, matrix products, contract_rows(): lax.dot_general(left, right, (((0,), (0,)), ((), ())), preferred_element_...  16 us
  transfers between devices with their start and end apart: 15, of which 7 were waited for; matrix products, arithmetic and copies ran while one was open for 22% of the time, Pallas kernels for 0%

profile of v1, /device:TPU:0, one launch (start us, length us, event | category | flops | bytes accessed | tf_op | source)
XLA Modules:
  0.0 766.1 jit_solution(15131227517994452526)
XLA Ops:
  10.4 10.1 %all-gather = bf16[1,2,3,64]{2,1,0,3:T(2,128)(2,1)S(1)} all-gather(bf16[1,2,3,8]{2,1,0,3:T(2,128)(2,1)S(1)} %copy.178), channel_id=2, replica_groups=mesh['dp'=8,'tensor'=4] {'dp'}, dimensions={3}, use_global_device_ids=true | all-gather | bytes 864 | tf_op jit(solution)/shard_map/all_gather | solution.py:98
  23.0 1.5 collective-permute-start.1
  25.9 12.6 %all-gather.1 = bf16[1,192,768]{1,0,2:T(2,128)(2,1)S(1)} all-gather(bf16[1,192,96]{1,0,2:T(2,128)(2,1)S(1)} %copy.139), channel_id=3, replica_groups=mesh['dp'=8,'tensor'=4] {'dp'}, dimensions={2}, use_global_device_ids=true | all-gather | bytes 331776 | tf_op jit(solution)/shard_map/all_gather | solution.py:99
  39.0 1.3 broadcast_select_fusion.3
  41.1 1.5 broadcast_compare_fusion
  42.6 13.4 %collective-permute-done.2 = bf16[4,96,3,192]{3,1,2,0:T(8,128)(2,1)S(1)} collective-permute-done((bf16[4,96,3,192]{3,1,2,0:T(8,128)(2,1)S(1)}, bf16[4,96,3,192]{3,1,2,0:T(8,128)(2,1)S(1)}, u32[]{:S(2)}, u32[]{:S(2)}) %collective-permute-start.2) | collective-permute-done | bytes 442400 | tf_op jit(solution)/shard_map/ppermute | solution.py:28
  57.4 2.6 copy.130
  60.0 2.9 reshape.217
  62.9 4.6 fusion.13
  67.5 6.2 reshape.218
  73.6 2.4 fusion.69
  76.1 4.4 fusion.73
  80.5 1.8 fusion
  82.4 2.8 copy-done
  85.3 2.8 fusion.23
  89.8 2.7 convolution_convert_fusion.2
  92.6 1.6 slice.205
  94.3 1.6 slice.204
  98.2 8.4 %all-gather.4 = bf16[1,6,128]{1,0,2:T(2,128)(2,1)S(1)} all-gather(bf16[1,6,16]{1,0,2:T(2,128)(2,1)} %copy.142), channel_id=6, replica_groups=mesh['dp'=8,'tensor'=4] {'dp'}, dimensions={2}, use_global_device_ids=true | all-gather | bytes 1728 | tf_op jit(solution)/shard_map/all_gather | solution.py:101
  108.0 10.3 %all-gather.2 = bf16[1,6,768]{1,0,2:T(2,128)(2,1)S(1)} all-gather(bf16[1,6,96]{1,0,2:T(2,128)(2,1)S(1)} %copy.182), channel_id=4, replica_groups=mesh['dp'=8,'tensor'=4] {'dp'}, dimensions={2}, use_global_device_ids=true | all-gather | bytes 10368 | tf_op jit(solution)/shard_map/all_gather | solution.py:103
  118.7 13.0 %slice_reduce_fusion.1 = (f32[768]{0:T(1024)S(1)}, f32[768]{0:T(1024)S(1)}, f32[768]{0:T(1024)S(1)}, f32[768]{0:T(1024)S(1)}, f32[768]{0:T(1024)S(1)}, /*index=5*/f32[768]{0:T(1024)S(1)}) fusion(f32[1,6,768]{1,0,2:T(1,128)S(1)} %convert_element_type.170), kind=kLoop, calls=%fused_computation.82 | loop fusion | bytes 36864 | tf_op jit(solution)/shard_map/slice | solution.py:142
  131.7 82.3 %all-reduce.6.cloned.1.call-done = bf16[2048,768]{1,0:T(8,128)(2,1)} async-done(((bf16[2048,768]{1,0:T(8,128)(2,1)}), bf16[2048,768]{1,0:T(8,128)(2,1)}) %all-reduce.6.cloned.1.call-update) | async-done | bytes 3145744 | tf_op jit(solution)/shard_map/psum | solution.py:134
  214.0 3.1 fusion.11
  217.1 3.6 multiply_reduce_fusion.4
  220.8 7.4 multiply_convert_fusion.1
  228.3 6.2 convolution_convert_fusion.1
  234.5 120.2 %all-reduce.8.cloned.1.call-done = bf16[2048,768]{1,0:T(8,128)(2,1)} async-done(((bf16[2048,768]{1,0:T(8,128)(2,1)}), bf16[2048,768]{1,0:T(8,128)(2,1)}) %all-reduce.8.cloned.1.call-update) | async-done | bytes 3145744 | tf_op jit(solution)/shard_map/psum | solution.py:141
  354.7 4.9 fusion.67
  361.5 3.0 fusion.7
  364.6 4.3 fusion.66
  369.0 5.9 convert_reduce_fusion.1
  374.9 1.7 copy-done.38
  376.7 4.0 convolution_convert_fusion
  381.6 8.0 %fusion.60 = f32[768,768]{0,1:T(8,128)} fusion(bf16[2048,768]{1,0:T(8,128)(2,1)} %copy-done.39, f32[2048,768]{1,0:T(8,128)} %copy-done.2, f32[2048]{0:T(1024)S(1)} %negate_multiply_fusion.1), kind=kOutput, calls=%fused_computation.156 | convolution fusion | flops 2419064832 | bytes 11804672 | tf_op jit(solution)/shard_map/dot_general | solution.py:64
  389.7 8.0 %fusion.61 = f32[768,768]{1,0:T(8,128)} fusion(bf16[2048,768]{1,0:T(8,128)(2,1)} %copy-done.38, f32[2048,768]{1,0:T(8,128)} %get-tuple-element.123, f32[768]{0:T(1024)} %copy-done.27, f32[768]{0:T(1024)} %copy-done.24, f32[2048]{0:T(1024)S(1)} %fusion.49), kind=kOutput, calls=%fused_computation.157 | convolution fusion | flops 2422210560 | bytes 11810816 | tf_op jit(solution)/shard_map/dot_general | solution.py:64
  397.8 103.1 %all-reduce.10.cloned.1.call-done = bf16[2048,768]{1,0:T(8,128)(2,1)} async-done(((bf16[2048,768]{1,0:T(8,128)(2,1)}), bf16[2048,768]{1,0:T(8,128)(2,1)}) %all-reduce.10.cloned.1.call-update) | async-done | bytes 3145744 | tf_op jit(solution)/shard_map/psum | solution.py:151
  500.9 8.2 %multiply_reduce_fusion.1 = (f32[768]{0:T(1024)}, f32[2048]{0:T(1024)S(1)}, f32[768]{0:T(1024)}, f32[768]{0:T(1024)}) fusion(f32[2048,768]{1,0:T(8,128)} %get-tuple-element.123, f32[2048]{0:T(1024)S(1)} %fusion.49, bf16[2048,768]{1,0:T(8,128)(2,1)} %all-reduce.10.cloned.1.call-done, f32[2048,768]{1,0:T(8,128)} %copy-done.2, ...), kind=kLoop, calls=%fused_computation.19 | loop fusion | flops 17297152 | bytes 15765504 | tf_op jit(solution)/shard_map/transpose(jvp())/reduce_sum | solution.py:48
  509.1 6.1 fusion.65
  515.2 2.6 copy-done.3
  517.8 2.2 convolution_convert_fusion.3
  520.0 3.0 reshape.221
  523.0 8.3 %multiply_reduce_fusion = (f32[4,3,512]{2,1,0:T(4,128)S(1)}, f32[4,3,512,512]{2,3,1,0:T(8,128)S(1)}) fusion(f32[4,3,512,512]{2,3,1,0:T(8,128)} %copy-done, f32[4,3,512]{2,1,0:T(4,128)S(1)} %log_add_fusion, bf16[4,512,1,3,64]{1,0,4,3,2:T(4,128)(2,1)} %copy-done.11, bf16[4,512,3,64]{1,0,3,2:T(4,128)(2,1)} %reshape.221), kind=kOutput, calls=%fused_computation.1 | convolution fusion | flops 412084224 | bytes 26787840 | tf_op jit(solution)/shard_map/bqhd,bkhd->bhqk/dot_general | solution.py:162
  531.3 6.9 multiply_convert_fusion
  538.2 2.6 copy-done.1
  541.9 1.5 copy.146
  543.4 3.2 stack.101
  546.6 5.1 fusion.22
  551.7 1.5 copy.148
  553.2 2.8 stack.102
  556.0 2.1 constant_dynamic-update-slice_fusion.2
  558.1 5.6 convolution_bitcast_fusion
  563.7 7.8 %fusion.18 = bf16[4,512,3,64]{1,3,2,0:T(8,128)(2,1)} fusion(f32[4,3,512,512]{2,3,1,0:T(8,128)} %copy-done, f32[4,3,512]{2,1,0:T(4,128)S(1)} %log_add_fusion, bf16[4,512,3,64]{1,0,3,2:T(4,128)(2,1)} %reshape.221), kind=kOutput, calls=%fused_computation.54 | convolution fusion | flops 409337856 | bytes 14180352 | tf_op jit(solution)/shard_map/bhqk,bqhd->bkhd/dot_general | solution.py:163
  571.6 2.1 constant_dynamic-update-slice_fusion.1
  573.6 2.6 copy.151
  576.3 2.8 stack.103
  579.1 2.1 constant_dynamic-update-slice_fusion
  581.2 5.8 fusion.74
  587.0 2.8 copy.176
  591.2 6.2 bitcast_convert_fusion
  606.9 14.3 %all-reduce = f32[2,3,64]{2,1,0:T(4,128)S(1)} all-reduce(f32[2,3,64]{2,1,0:T(4,128)S(1)} %reshape.223), channel_id=9, replica_groups=mesh['dp'=8,'tensor'=4] {'dp'}, use_global_device_ids=true, to_apply=%region_17.18.clone | all-reduce | flops 384 | bytes 3072
  629.2 19.7 %reduce-scatter.20.cloned.1.call-done = f32[96,576]{1,0:T(8,128)} async-done(((f32[768,576]{1,0:T(8,128)}), f32[96,576]{1,0:T(8,128)}) %reduce-scatter.20.cloned.1.call-update) | async-done | bytes 221200
  650.1 67.7 %all-reduce.12.cloned.1.call-done = bf16[2048,768]{1,0:T(8,128)(2,1)} async-done(((bf16[2048,768]{1,0:T(8,128)(2,1)}), bf16[2048,768]{1,0:T(8,128)(2,1)}) %all-reduce.12.cloned.1.call-update) | async-done | bytes 3145744 | tf_op jit(solution)/shard_map/psum | solution.py:182
  717.9 5.4 add_reduce_fusion
  726.3 31.0 %reduce-scatter.26.cloned.1.call-done = f32[96,6]{1,0:T(8,128)} async-done(((f32[768,6]{1,0:T(8,128)}), f32[96,6]{1,0:T(8,128)}) %reduce-scatter.26.cloned.1.call-update) | async-done | bytes 2320
  (196 shorter events, 42.0 us)
Async XLA Ops:
  8.0 33.1 %copy-start.26 = (s32[4,512]{1,0:T(4,128)S(1)}, s32[4,512]{1,0:T(4,128)}, u32[]{:S(2)}) copy-start(s32[4,512]{1,0:T(4,128)} %param.13) | copy-start | bytes 24580
  8.0 205.9 %all-reduce.6.cloned.1.call-start = ((), (), s32[]{:S(2)}) async-start(), calls=%async_computation.6 | async-start | bytes 6291456 | tf_op jit(solution)/shard_map/psum | solution.py:134
  9.1 11.5 %collective-permute-start = (bf16[1,96,3,192]{3,1,2,0:T(8,128)(2,1)S(1)}, bf16[1,96,3,192]{3,1,2,0:T(8,128)(2,1)S(1)}, u32[]{:S(2)}, u32[]{:S(2)}) collective-permute-start(bf16[1,96,3,192]{3,1,2,0:T(8,128)(2,1)S(1)} %slice.206), channel_id=1, source_target_pairs={{0,4},{4,0},{8,12},{12,8},{16,20},{20,16},{24,28},{28,24},{1,5},{5... | collective-permute-start | bytes 331784 | tf_op jit(solution)/shard_map/ppermute | solution.py:28
  21.5 0.7 copy-start.14
  21.5 1.4 copy-start.15
  23.0 16.0 %collective-permute-start.1 = (bf16[2,96,3,192]{3,1,2,0:T(8,128)(2,1)}, bf16[2,96,3,192]{3,1,2,0:T(8,128)(2,1)}, u32[]{:S(2)}, u32[]{:S(2)}) collective-permute-start(bf16[2,96,3,192]{3,1,2,0:T(8,128)(2,1)} %pad_maximum_fusion.5), channel_id=1, source_target_pairs={{0,8},{4,12},{8,0},{12,4},{16,24},{20,28},{24,16},{28,20},{1,9},{5... | collective-permute-start | bytes 663560 | tf_op jit(solution)/shard_map/ppermute | solution.py:28
  39.0 23.9 %copy-start.6 = (bf16[4,512,768]{2,1,0:T(8,128)(2,1)S(1)}, bf16[4,512,768]{2,1,0:T(8,128)(2,1)}, u32[]{:S(2)}) copy-start(bf16[4,512,768]{2,1,0:T(8,128)(2,1)} %param.11) | copy-start | bytes 9437188
  40.4 15.7 %collective-permute-start.2 = (bf16[4,96,3,192]{3,1,2,0:T(8,128)(2,1)S(1)}, bf16[4,96,3,192]{3,1,2,0:T(8,128)(2,1)S(1)}, u32[]{:S(2)}, u32[]{:S(2)}) collective-permute-start(bf16[4,96,3,192]{3,1,2,0:T(8,128)(2,1)S(1)} %pad_maximum_fusion.1), channel_id=1, source_target_pairs={{0,16},{4,20},{8,24},{12,28},{16,0},{20,4},{24,8},{28,12},{1,17},{... | collective-permute-start | bytes 1327112 | tf_op jit(solution)/shard_map/ppermute | solution.py:28
  76.1 4.4 copy-start.9
  76.1 4.4 copy-start.12
  76.1 6.3 copy-start.11
  80.5 4.7 copy-start
  80.5 4.7 copy-start.18
  82.3 5.8 copy-start.20
  88.9 0.9 copy-start.8
  92.5 128.3 %all-gather.9.cloned.1.call-start = ((), (), s32[]{:S(2)}) async-start(), calls=%async_computation.12 | async-start | bytes 1327104 | tf_op jit(solution)/shard_map/all_gather | solution.py:100
  94.2 134.1 %all-gather.11.cloned.1.call-start = ((), (), s32[]{:S(2)}) async-start(), calls=%async_computation.13 | async-start | bytes 1327104 | tf_op jit(solution)/shard_map/all_gather | solution.py:102
  95.9 258.8 %all-reduce.8.cloned.1.call-start = ((), (), s32[]{:S(2)}) async-start(), calls=%async_computation.7 | async-start | bytes 6291456 | tf_op jit(solution)/shard_map/psum | solution.py:141
  131.7 223.0 %copy-start.24 = (f32[768]{0:T(1024)}, f32[768]{0:T(1024)S(1)}, u32[]{:S(2)}) copy-start(f32[768]{0:T(1024)S(1)} %get-tuple-element.111) | copy-start | bytes 9220
  131.7 223.0 %copy-start.27 = (f32[768]{0:T(1024)}, f32[768]{0:T(1024)S(1)}, u32[]{:S(2)}) copy-start(f32[768]{0:T(1024)S(1)} %get-tuple-element.110) | copy-start | bytes 9220
  214.0 3.2 copy-start.7
  220.8 7.5 copy-start.22
  228.3 6.2 copy-start.39
  234.5 266.4 %all-reduce.10.cloned.1.call-start = ((), (), s32[]{:S(2)}) async-start(), calls=%async_computation.8 | async-start | bytes 6291456 | tf_op jit(solution)/shard_map/psum | solution.py:151
  359.6 1.9 copy-start.4
  361.5 7.4 slice-start
  364.6 4.3 copy-start.37
  364.6 4.3 slice-start.1
  368.9 6.0 copy-start.2
  369.0 7.7 %copy-start.36 = (bf16[1,768,768]{2,1,0:T(8,128)(2,1)S(1)}, bf16[1,768,768]{2,1,0:T(8,128)(2,1)}, u32[]{:S(2)}) copy-start(bf16[1,768,768]{2,1,0:T(8,128)(2,1)} %all-gather.9.cloned.1.call-done) | copy-start | bytes 3538948
  374.9 1.8 copy-start.38
  380.7 222.2 %reduce-scatter.24.cloned.1.call-start = ((), (), s32[]{:S(2)}) async-start(), calls=%async_computation.16 | async-start | bytes 73728
  381.5 8.1 %copy-start.19 = (f32[4,3,512]{2,1,0:T(4,128)S(1)}, f32[4,3,512]{2,1,0:T(4,128)}, u32[]{:S(2)}) copy-start(f32[4,3,512]{2,1,0:T(4,128)} %copy-done.18) | copy-start | bytes 73732
  381.5 8.1 %copy-start.21 = (f32[4,3,512]{2,1,0:T(4,128)S(1)}, f32[4,3,512]{2,1,0:T(4,128)}, u32[]{:S(2)}) copy-start(f32[4,3,512]{2,1,0:T(4,128)} %copy-done.20) | copy-start | bytes 73732
  381.5 241.7 %reduce-scatter.18.cloned.1.call-start = ((), (), s32[]{:S(2)}) async-start(), calls=%async_computation.11 | async-start | bytes 2654208 | tf_op jit(solution)/shard_map/reduce_scatter | solution.py:191
  389.6 235.8 %reduce-scatter.16.cloned.1.call-start = ((), (), s32[]{:S(2)}) async-start(), calls=%async_computation.10 | async-start | bytes 2654208 | tf_op jit(solution)/shard_map/reduce_scatter | solution.py:189
  389.7 111.2 %copy-start.25 = (f32[768]{0:T(1024)S(1)}, f32[768]{0:T(1024)}, u32[]{:S(2)}) copy-start(f32[768]{0:T(1024)} %copy-done.24) | copy-start | bytes 9220
  397.7 111.4 %copy-start.23 = (f32[2048]{0:T(1024)S(1)}, f32[2048]{0:T(1024)}, u32[]{:S(2)}) copy-start(f32[2048]{0:T(1024)} %copy-done.22) | copy-start | bytes 24580
  397.7 229.7 %reduce-scatter.22.cloned.1.call-start = ((), (), s32[]{:S(2)}) async-start(), calls=%async_computation.15 | async-start | bytes 884736
  500.9 8.2 %copy-start.5 = (bf16[2048,768]{1,0:T(8,128)(2,1)S(1)}, bf16[2048,768]{1,0:T(8,128)(2,1)}, u32[]{:S(2)}) copy-start(bf16[2048,768]{1,0:T(8,128)(2,1)} %all-reduce.10.cloned.1.call-done) | copy-start | bytes 9437188
  515.2 2.6 copy-start.3
  531.3 9.5 %copy-start.13 = (bf16[4,512,1,3,64]{1,0,4,3,2:T(4,128)(2,1)S(1)}, bf16[4,512,1,3,64]{1,0,4,3,2:T(4,128)(2,1)}, u32[]{:S(2)}) copy-start(bf16[4,512,1,3,64]{1,0,4,3,2:T(4,128)(2,1)} %copy-done.12) | copy-start | bytes 2359300
  538.2 2.6 copy-start.1
  571.5 77.4 %reduce-scatter.20.cloned.1.call-start = ((), (), s32[]{:S(2)}) async-start(), calls=%async_computation.14 | async-start | bytes 2211840
  589.9 128.0 %all-reduce.12.cloned.1.call-start = ((), (), s32[]{:S(2)}) async-start(), calls=%async_computation.9 | async-start | bytes 6291456 | tf_op jit(solution)/shard_map/psum | solution.py:182
  591.2 8.3 %copy-start.30 = (f32[768]{0:T(1024)S(1)}, f32[768]{0:T(1024)}, u32[]{:S(2)}) copy-start(f32[768]{0:T(1024)} %convert_reduce_fusion) | copy-start | bytes 9220
  591.2 11.7 %copy-start.28 = (f32[768]{0:T(1024)S(1)}, f32[768]{0:T(1024)}, u32[]{:S(2)}) copy-start(f32[768]{0:T(1024)} %get-tuple-element.104) | copy-start | bytes 9220
  591.2 15.2 %copy-start.29 = (f32[768]{0:T(1024)S(1)}, f32[768]{0:T(1024)}, u32[]{:S(2)}) copy-start(f32[768]{0:T(1024)} %get-tuple-element.107) | copy-start | bytes 9220
  597.4 9.0 %copy-start.10 = (bf16[2048,3,192]{0,2,1:T(8,128)(2,1)S(1)}, bf16[2048,3,192]{0,2,1:T(8,128)(2,1)}, u32[]{:S(2)}) copy-start(bf16[2048,3,192]{0,2,1:T(8,128)(2,1)} %constant_dynamic-update-slice_fusion) | copy-start | bytes 7077892
  597.5 31.0 %copy-start.17 = (f32[3,192,96]{2,1,0:T(8,128)S(1)}, f32[3,192,96]{2,1,0:T(8,128)}, u32[]{:S(2)}) copy-start(f32[3,192,96]{2,1,0:T(8,128)} %param.17) | copy-start | bytes 663556
  597.5 159.8 %reduce-scatter.26.cloned.1.call-start = ((), (), s32[]{:S(2)}) async-start(), calls=%async_computation.17 | async-start | bytes 442368
  603.7 119.5 %copy-start.31 = (f32[6,16]{1,0:T(8,128)}, f32[6,16]{1,0:T(8,128)S(1)}, u32[]{:S(2)}) copy-start(f32[6,16]{1,0:T(8,128)S(1)} %copy.173) | copy-start | bytes 1156
  622.0 101.3 %copy-start.33 = (f32[2,3,8]{2,0,1:T(2,128)}, f32[2,3,8]{2,0,1:T(2,128)S(1)}, u32[]{:S(2)}) copy-start(f32[2,3,8]{2,0,1:T(2,128)S(1)} %get-tuple-element.115) | copy-start | bytes 580
  628.5 94.8 %copy-start.16 = (f32[192,96]{1,0:T(8,128)}, f32[192,96]{1,0:T(8,128)S(1)}, u32[]{:S(2)}) copy-start(f32[192,96]{1,0:T(8,128)S(1)} %copy.171) | copy-start | bytes 221188
  650.1 73.2 %copy-start.34 = (f32[1,768]{1,0:T(1,128)S(1)}, f32[1,768]{1,0:T(1,128)}, u32[]{:S(2)}) copy-start(f32[1,768]{1,0:T(1,128)} %reshape.228) | copy-start | bytes 9220
  650.1 108.0 %copy-start.35 = (f32[3,6,96]{2,1,0:T(8,128)S(1)}, f32[3,6,96]{2,1,0:T(8,128)}, u32[]{:S(2)}) copy-start(f32[3,6,96]{2,1,0:T(8,128)} %param.21) | copy-start | bytes 20740
  758.2 0.6 copy-start.32
Sparse Core Ops, SparseCore 0:
  92.6 121.2 all-reduce.5
  234.6 120.0 all-reduce.7
  380.8 120.0 all-reduce.9
  597.6 120.2 all-reduce.11
Sparse Core Ops, SparseCore 1:
  95.5 25.1 all-gather.8
  122.9 23.8 all-gather.10
  384.8 32.5 reduce-scatter.23
  421.2 42.2 reduce-scatter.17
  467.4 42.2 reduce-scatter.15
  571.6 33.9 reduce-scatter.21
  608.8 40.0 reduce-scatter.19
  724.4 32.9 reduce-scatter.25
